TPU v7x, 256 devices: a whole 4x4x8 slice. The times are simulated.
256 devices in a mesh: pair: 8 (over x_lo, y), outv: 8 (over z), conv: 4 (over x_hi, core).
Axes of the slice: x: 4 (x_hi: 2, x_lo: 2; x = x_hi * 2 + x_lo), y: 4, z: 8, core: 2. Of those that a mesh axis runs over, the one named last changes fastest.
Arguments:
- amplitudes: bfloat16 [16384, 6144], P('pair', ('conv', 'outv')), may hold values from -6 to 6
- integrals: bfloat16 [6144, 12288], P('conv', ('outv', 'pair')), may hold values from -0.21875 to 0.21875
- amp_mask: int32 [8, 64], P('pair', 'conv'), may hold values from 0 to 1, as said below
- int_mask: int32 [64, 128], P('conv', 'outv'), may hold values 0 or 1
Outputs:
- ladder: bfloat16 [12288, 16384], P(('outv', 'conv'), 'pair')
Inputs may be any that keep to these rules, and one draw needn't show every extreme that they name: `amp_mask`: 0 or 1; the share of ones differs from pair tile to pair tile.
All inputs are finite; a program needn't handle non-finite values. No bound on the sum of `int_mask` on one device may be relied on, other than what follows from the above.
Results may differ from a plain program's by a relative error of at most 0.001.
Values may be sent and summed in bfloat16 or wider, within the bound.
No kernel may reach another device: no remote copies, remote signals or barrier semaphores. Data moves between devices by JAX's collectives and lax.ppermute only.
A program may use at most 64 MiB of HBM per device.

v0:
```python
import jax
import jax.numpy as jnp
from jax import lax
from jax.sharding import PartitionSpec as P

TW = 96


def column_mask(block_mask, first, width):
    tiles = block_mask.shape[1]
    col_tile = (first * width + jnp.arange(width, dtype=jnp.int32)) // TW
    onehot = (col_tile[None, :] == jnp.arange(tiles, dtype=jnp.int32)[:, None]).astype(jnp.float32)
    return jnp.dot(block_mask.astype(jnp.float32), onehot, preferred_element_type=jnp.float32)


def contract(columns, amp_rows):
    dims = (((0,), (1,)), ((), ()))
    return lax.dot_general(columns, amp_rows, dims, preferred_element_type=jnp.float32)


def body(amplitudes, integrals, amp_mask, int_mask):
    width_amp = amplitudes.shape[1]
    amp_cols = column_mask(amp_mask, lax.axis_index("outv"), width_amp)
    amp_local = amplitudes * amp_cols.astype(jnp.bfloat16)
    amp_rows = lax.all_gather(amp_local, "outv", axis=1, tiled=True)
    tiles_k = int_mask.shape[0]
    width_int = integrals.shape[1]
    int_cols = column_mask(int_mask, lax.axis_index("pair"), width_int)
    int_local = (
        integrals.reshape(tiles_k, TW, width_int) * int_cols[:, None, :].astype(jnp.bfloat16)
    ).reshape(tiles_k * TW, width_int)
    int_full = lax.all_gather(int_local, "pair", axis=1, tiled=True)
    summed = lax.psum_scatter(contract(int_full, amp_rows), "conv", scatter_dimension=0, tiled=True)
    return summed.astype(jnp.bfloat16)


def solution(mesh):
    placed = (
        P("pair", ("conv", "outv")),
        P("conv", ("outv", "pair")),
        P("pair", "conv"),
        P("conv", "outv"),
    )
    return jax.shard_map(
        body, mesh=mesh, in_specs=placed, out_specs=P(("outv", "conv"), "pair"), check_vma=False
    )
```

profile of v0, /device:TPU:1, one launch (start us, length us, event | category | flops | bytes accessed | tf_op | source)
XLA Modules:
  0.0 285.8 jit_solution(13967554948303165017)
XLA Ops:
  6.5 0.0 all-gather.3.cloned.1.call-start
  6.6 0.8 fusion
  7.4 0.1 copy.5
  7.5 0.5 mul.26
  8.0 0.9 mul.27
  8.9 2.0 mul.28
  10.9 0.0 all-gather.3.cloned.1.call-update
  10.9 0.0 all-gather.5.cloned.1.call-start
  11.0 0.8 fusion.1
  11.8 2.1 broadcast_multiply_fusion
  13.9 0.0 all-gather.5.cloned.1.call-update
  13.9 0.0 reduce-scatter.2.cloned.1.call-start
  14.0 61.0 %all-gather.3.cloned.1.call-done = bf16[1536,1536]{0,1:T(8,128)(2,1)} async-done(((bf16[1536,192]{0,1:T(8,128)(2,1)}), bf16[1536,1536]{0,1:T(8,128)(2,1)}) %all-gather.3.cloned.1.call-update) | async-done | bytes 4718608 | tf_op jit(solution)/shard_map/all_gather | solution.py:32
  75.0 75.1 %all-gather.5.cloned.1.call-done = bf16[2048,1536]{0,1:T(8,128)(2,1)} async-done(((bf16[2048,192]{0,1:T(8,128)(2,1)}), bf16[2048,1536]{0,1:T(8,128)(2,1)}) %all-gather.5.cloned.1.call-update) | async-done | bytes 6291472 | tf_op jit(solution)/shard_map/all_gather | solution.py:25
  150.1 16.1 %fusion.5 = f32[1536,2048]{1,0:T(8,128)} fusion(bf16[1536,1536]{0,1:T(8,128)(2,1)} %all-gather.3.cloned.1.call-done, bf16[2048,1536]{0,1:T(8,128)(2,1)} %all-gather.5.cloned.1.call-done), kind=kOutput, calls=%fused_computation.12 | convolution fusion | flops 9663676416 | bytes 23592960 | tf_op jit(solution)/shard_map/dot_general | solution.py:18
  166.2 0.0 reduce-scatter.2.cloned.1.call-update
  166.2 109.8 %reduce-scatter.2.cloned.1.call-done = f32[384,2048]{1,0:T(8,128)} async-done(((f32[1536,2048]{1,0:T(8,128)}), f32[384,2048]{1,0:T(8,128)}) %reduce-scatter.2.cloned.1.call-update) | async-done | bytes 3145744 | tf_op jit(solution)/shard_map/reduce_scatter | solution.py:33
  276.0 3.3 %convert_element_type.27 = bf16[384,2048]{1,0:T(8,128)(2,1)} convert(f32[384,2048]{1,0:T(8,128)} %reduce-scatter.2.cloned.1.call-done) | non-fusion elementwise | flops 786432 | bytes 4718592 | tf_op jit(solution)/shard_map/convert_element_type | solution.py:34
  (3 shorter events, 0.0 us)
Async XLA Ops:
  6.5 68.4 %all-gather.3.cloned.1.call-start = ((), (), s32[]{:S(2)}) async-start(), calls=%async_computation.1 | async-start | bytes 5308416 | tf_op jit(solution)/shard_map/all_gather | solution.py:32
  10.9 139.1 %all-gather.5.cloned.1.call-start = ((), (), s32[]{:S(2)}) async-start(), calls=%async_computation.2 | async-start | bytes 7077888 | tf_op jit(solution)/shard_map/all_gather | solution.py:25
  13.9 262.1 %reduce-scatter.2.cloned.1.call-start = ((), (), s32[]{:S(2)}) async-start(), calls=%async_computation.3 | async-start | bytes 15728640 | tf_op jit(solution)/shard_map/reduce_scatter | solution.py:33
Sparse Core Ops, SparseCore 0:
  11.0 63.8 all-gather.2
  76.7 73.2 all-gather.4
  166.3 109.6 reduce-scatter.1
where the time goes:
time: 286 us
  waiting for transfers between devices  246 us (86%)
  matrix products  17.7 us (6%)
  between operations  13.1 us (5%)
  other arithmetic  7.46 us (3%)
    reduce_scatter x1, waiting for transfers between devices, body(): lax.psum_scatter(contract(int_full, amp_rows), 'conv', scatter_dimension=...  110 us
    all_gather x1, waiting for transfers between devices, body(): amp_rows = lax.all_gather(amp_local, 'outv', axis=1, tiled=True)  75.1 us
    all_gather x1, waiting for transfers between devices, body(): int_full = lax.all_gather(int_local, 'pair', axis=1, tiled=True)  61 us
    dot_general x1, matrix products, contract(): lax.dot_general(columns, amp_rows, dims, preferred_element_type=jnp.float32)  16.1 us
  transfers between devices with their start and end apart: 3, of which 3 were waited for; matrix products, arithmetic and copies ran while one was open for 1% of the time, Pallas kernels for 0%

commit v1 on v0

--- a/solution.py
+++ b/solution.py
@@ -22,7 +22,8 @@
     width_amp = amplitudes.shape[1]
     amp_cols = column_mask(amp_mask, lax.axis_index("outv"), width_amp)
     amp_local = amplitudes * amp_cols.astype(jnp.bfloat16)
-    amp_rows = lax.all_gather(amp_local, "outv", axis=1, tiled=True)
+    local_next = jnp.concatenate(lax.axis_size("outv") * [amp_local], axis=1)
+    amp_rows = lax.all_to_all(local_next, "outv", 1, 1, tiled=True)
     tiles_k = int_mask.shape[0]
     width_int = integrals.shape[1]
     int_cols = column_mask(int_mask, lax.axis_index("pair"), width_int)

time: 286 us -> 301 us (1.052)
  starting transfers between devices: 0.09 us -> 9.22 us
    all_to_all x0 -> x1, waiting for transfers between devices: none -> 77.1 us  [body(): amp_rows = lax.all_to_all(local_next, 'outv', 1, 1, tiled=True)]
    all_gather x1 -> x0, waiting for transfers between devices: 75.1 us -> none  [body(): amp_rows = lax.all_gather(amp_local, 'outv', axis=1, tiled=True)]
    all_to_all x0 -> x1, starting transfers between devices: none -> 9.15 us  [body(): amp_rows = lax.all_to_all(local_next, 'outv', 1, 1, tiled=True)]
    unnamed x0 -> x7, other arithmetic: none -> 5.93 us
where the time goes in v1:
time: 301 us
  waiting for transfers between devices  247 us (82%)
  matrix products  17 us (6%)
  between operations  13.5 us (4%)
  other arithmetic  10.4 us (3%)
  starting transfers between devices  9.22 us (3%)
  local copies, waits for them, and re-layouts  4.15 us (1%)
    reduce_scatter x1, waiting for transfers between devices, body(): lax.psum_scatter(contract(int_full, amp_rows), 'conv', scatter_dimension=...  107 us
    all_to_all x1, waiting for transfers between devices, body(): amp_rows = lax.all_to_all(local_next, 'outv', 1, 1, tiled=True)  77.1 us
    all_gather x1, waiting for transfers between devices, body(): int_full = lax.all_gather(int_local, 'pair', axis=1, tiled=True)  62.1 us
    dot_general x1, matrix products, contract(): lax.dot_general(columns, amp_rows, dims, preferred_element_type=jnp.float32)  16 us
    all_to_all x1, starting transfers between devices, body(): amp_rows = lax.all_to_all(local_next, 'outv', 1, 1, tiled=True)  9.15 us
  transfers between devices with their start and end apart: 3, of which 3 were waited for; matrix products, arithmetic and copies ran while one was open for 1% of the time, Pallas kernels for 0%

profile of v1, /device:TPU:1, one launch (start us, length us, event | category | flops | bytes accessed | tf_op | source)
XLA Modules:
  0.0 300.9 jit_solution(13848429879386298907)
XLA Ops:
  6.5 0.0 copy-start
  6.5 0.9 fusion.1
  7.4 1.3 constant_dynamic-update-slice_fusion.7
  8.7 1.3 constant_dynamic-update-slice_fusion.6
  10.1 1.3 constant_dynamic-update-slice_fusion.5
  11.4 1.3 constant_dynamic-update-slice_fusion.4
  12.7 0.0 copy-done
  12.8 0.2 constant_dynamic-update-slice_fusion.3
  13.0 0.2 constant_dynamic-update-slice_fusion.2
  13.2 0.2 constant_dynamic-update-slice_fusion.1
  13.4 0.2 constant_dynamic-update-slice_fusion
  13.6 0.0 copy-start.1
  13.6 2.7 copy-done.1
  16.2 0.0 copy-start.3
  16.2 0.0 copy-start.2
  16.2 9.1 %all-to-all-start = ((bf16[2048,8,192]{0,2,1:T(8,128)(2,1)}), bf16[2048,8,192]{0,2,1:T(8,128)(2,1)}, u32[]{:S(2)}, u32[]{:S(2)}) async-start(bf16[2048,8,192]{0,2,1:T(8,128)(2,1)} %bitcast.13), calls=%async_computation | async-start | bytes 12582912 | tf_op jit(solution)/shard_map/all_to_all | solution.py:26
  25.4 0.0 all-gather.2.cloned.1.call-start
  25.5 0.0 copy-done.3
  25.5 0.1 fusion
  25.6 0.1 copy.5
  25.7 0.5 mul.26
  26.2 0.9 mul.27
  27.1 0.0 copy-done.2
  27.1 1.0 mul.28
  28.0 0.0 all-gather.2.cloned.1.call-update
  28.1 0.0 reduce-scatter.2.cloned.1.call-start
  28.1 62.1 %all-gather.2.cloned.1.call-done = bf16[1536,1536]{0,1:T(8,128)(2,1)} async-done(((bf16[1536,192]{0,1:T(8,128)(2,1)}), bf16[1536,1536]{0,1:T(8,128)(2,1)}) %all-gather.2.cloned.1.call-update) | async-done | bytes 4718608 | tf_op jit(solution)/shard_map/all_gather | solution.py:33
  90.2 77.1 %all-to-all-done = bf16[2048,8,192]{0,2,1:T(8,128)(2,1)} async-done(((bf16[2048,8,192]{0,2,1:T(8,128)(2,1)}), bf16[2048,8,192]{0,2,1:T(8,128)(2,1)}, u32[]{:S(2)}, u32[]{:S(2)}) %all-to-all-start) | async-done | bytes 6291488 | tf_op jit(solution)/shard_map/all_to_all | solution.py:26
  167.4 16.0 %fusion.5 = f32[1536,2048]{1,0:T(8,128)} fusion(bf16[1536,1536]{0,1:T(8,128)(2,1)} %all-gather.2.cloned.1.call-done, bf16[2048,1536]{0,1:T(8,128)(2,1)} %bitcast.5), kind=kOutput, calls=%fused_computation.20 | convolution fusion | flops 9663676416 | bytes 23592960 | tf_op jit(solution)/shard_map/dot_general | solution.py:18
  183.4 0.0 reduce-scatter.2.cloned.1.call-update
  183.4 107.4 %reduce-scatter.2.cloned.1.call-done = f32[384,2048]{1,0:T(8,128)} async-done(((f32[1536,2048]{1,0:T(8,128)}), f32[384,2048]{1,0:T(8,128)}) %reduce-scatter.2.cloned.1.call-update) | async-done | bytes 3145744 | tf_op jit(solution)/shard_map/reduce_scatter | solution.py:34
  290.8 3.3 %convert_element_type.27 = bf16[384,2048]{1,0:T(8,128)(2,1)} convert(f32[384,2048]{1,0:T(8,128)} %reduce-scatter.2.cloned.1.call-done) | non-fusion elementwise | flops 786432 | bytes 4718592 | tf_op jit(solution)/shard_map/convert_element_type | solution.py:35
  (3 shorter events, 0.0 us)
Async XLA Ops:
  6.5 6.2 %copy-start = (bf16[2048,192]{0,1:T(8,128)(2,1)S(1)}, bf16[2048,192]{0,1:T(8,128)(2,1)}, u32[]{:S(2)}) copy-start(bf16[2048,192]{0,1:T(8,128)(2,1)} %param.4) | copy-start | bytes 2359300
  13.6 2.7 copy-start.1
  16.2 9.2 %copy-start.3 = (s32[16,16]{1,0:T(8,128)S(1)}, s32[16,16]{1,0:T(8,128)}, u32[]{:S(2)}) copy-start(s32[16,16]{1,0:T(8,128)} %param.7) | copy-start | bytes 3076
  16.2 10.8 %copy-start.2 = (bf16[1536,192]{0,1:T(8,128)(2,1)S(1)}, bf16[1536,192]{0,1:T(8,128)(2,1)}, u32[]{:S(2)}) copy-start(bf16[1536,192]{0,1:T(8,128)(2,1)} %param.5) | copy-start | bytes 1769476
  16.2 151.1 %all-to-all-start = ((bf16[2048,8,192]{0,2,1:T(8,128)(2,1)}), bf16[2048,8,192]{0,2,1:T(8,128)(2,1)}, u32[]{:S(2)}, u32[]{:S(2)}) async-start(bf16[2048,8,192]{0,2,1:T(8,128)(2,1)} %bitcast.13), calls=%async_computation | async-start | bytes 12582912 | tf_op jit(solution)/shard_map/all_to_all | solution.py:26
  25.4 64.8 %all-gather.2.cloned.1.call-start = ((), (), s32[]{:S(2)}) async-start(), calls=%async_computation.2 | async-start | bytes 5308416 | tf_op jit(solution)/shard_map/all_gather | solution.py:33
  28.1 262.8 %reduce-scatter.2.cloned.1.call-start = ((), (), s32[]{:S(2)}) async-start(), calls=%async_computation.3 | async-start | bytes 15728640 | tf_op jit(solution)/shard_map/reduce_scatter | solution.py:34
Sparse Core Ops, SparseCore 0:
  28.2 61.9 all-gather.1
  183.6 107.2 reduce-scatter.1
